TPU v7x, 32 devices: a whole 2x2x4 slice. The times are simulated.
32 devices in a mesh: dp: 4 (over z), row: 4 (over y, x), col: 2 (over core).
Axes of the slice: x: 2, y: 2, z: 4, core: 2. Of those that a mesh axis runs over, the one named last changes fastest.
Arguments:
- tokens: bfloat16 [16, 2048, 768], P(('dp', 'row'), 'col'), may hold values from -6 to 6
- timesteps: int32 [16], P(('dp', 'row')), may hold values from 0 to 999
- block_ids: int32 [16, 2048], P(('dp', 'row')), may hold values from 0 to 11, never falling along the last dimension, each value on 1 to 256 neighbouring positions
- table: float32 [1000, 768], replicated, may hold values from -3 to 3
- gain_one: float32 [768], replicated, may hold values from 0.5 to 1.5
- bias_one: float32 [768], replicated, may hold values from -1.75 to 1.75
- w_query: float32 [768, 768], P('row', 'col'), may hold values from -0.21875 to 0.21875
- w_key: float32 [768, 768], P('row', 'col'), may hold values from -0.21875 to 0.21875
- w_value: float32 [768, 768], P('row', 'col'), may hold values from -0.21875 to 0.21875
- b_query: float32 [768], P('col'), may hold values from -1.75 to 1.75
- b_value: float32 [768], P('col'), may hold values from -1.75 to 1.75
- w_out: float32 [768, 768], P('col', 'row'), may hold values from -3.5 to 3.5
- b_out: float32 [768], replicated, may hold values from -1.75 to 1.75
- gain_two: float32 [768], replicated, may hold values from 0.5 to 1.5
- bias_two: float32 [768], replicated, may hold values from -1.75 to 1.75
- w_up: float32 [768, 3072], P('row', 'col'), may hold values from -0.21875 to 0.21875
- b_up: float32 [3072], P('col'), may hold values from -1.75 to 1.75
- w_down: float32 [3072, 768], P('col', 'row'), may hold values from -0.109375 to 0.109375
- b_down: float32 [768], replicated, may hold values from -1.75 to 1.75
- cotangent: bfloat16 [16, 2048, 768], P(('dp', 'row'), 'col'), may hold values from -6 to 6
Outputs:
- layer_out: bfloat16 [16, 2048, 768], P(('dp', 'row'), 'col')
- grad_tokens: float32 [16, 2048, 768], P(('dp', 'row'), 'col')
- grad_table: float32 [1000, 768], replicated
- grad_gain_one: float32 [768], replicated
- grad_bias_one: float32 [768], replicated
- grad_w_query: float32 [768, 768], P('row', 'col')
- grad_w_key: float32 [768, 768], P('row', 'col')
- grad_w_value: float32 [768, 768], P('row', 'col')
- grad_b_query: float32 [768], P('col')
- grad_b_value: float32 [768], P('col')
- grad_w_out: float32 [768, 768], P('col', 'row')
- grad_b_out: float32 [768], replicated
- grad_gain_two: float32 [768], replicated
- grad_bias_two: float32 [768], replicated
- grad_w_up: float32 [768, 3072], P('row', 'col')
- grad_b_up: float32 [3072], P('col')
- grad_w_down: float32 [3072, 768], P('col', 'row')
- grad_b_down: float32 [768], replicated
Inputs may be any that keep to these rules, and one draw needn't show every extreme that they name: `block_ids`: block numbers never fall along a sequence; every block number of a sequence is used, each block holds 1 to 256 positions, and some block holds exactly 256.
All inputs are finite; a program needn't handle non-finite values.
Results may differ from a plain program's by a relative error of at most 0.012.
The roundings to bfloat16 on the way count: a program that leaves them out, or rounds other values in their place, can miss the bound.
Values may be sent and summed in bfloat16 or wider, within the bound.
No kernel may reach another device: no remote copies, remote signals or barrier semaphores. Data moves between devices by JAX's collectives and lax.ppermute only.
A program may use at most 256 MiB of HBM per device.

v0:
```python
import jax
import jax.numpy as jnp
from jax import lax
from jax.sharding import PartitionSpec as P

HEAD_DIM = 64
norm_eps = 1e-05
masked_score = -1000000000.0


def layer_norm_parts(values, gain, bias):
    mean = jnp.mean(values, axis=-1, keepdims=True)
    centred = values - mean
    inverse = lax.rsqrt(jnp.mean(centred * centred, axis=-1, keepdims=True) + norm_eps)
    unit = centred * inverse
    return (unit * gain + bias, unit, inverse)


def norm_back(grad_normed, unit, inverse, gain):
    grad_unit = grad_normed * gain
    first_mean = jnp.mean(grad_unit, axis=-1, keepdims=True)
    second_mean = jnp.mean(grad_unit * unit, axis=-1, keepdims=True)
    return inverse * (grad_unit - first_mean - unit * second_mean)


def gelu_exact(values):
    return jax.nn.gelu(values, approximate=False)


def shards(
    tokens,
    timesteps,
    block_ids,
    table,
    gain_one,
    bias_one,
    w_query,
    w_key,
    w_value,
    b_query,
    b_value,
    w_out,
    b_out,
    gain_two,
    bias_two,
    w_up,
    b_up,
    w_down,
    b_down,
    cotangent,
):
    seq_count, local_len, model_width = tokens.shape
    full_len = block_ids.shape[1]
    head_cols = w_query.shape[1]
    hidden_cols = w_up.shape[1]
    local_heads = head_cols // HEAD_DIM
    row_block = min(512, full_len)
    block_count = full_len // row_block
    scale_factor = HEAD_DIM ** (-0.5)
    col_index = lax.axis_index("col")
    row_index = lax.axis_index("row")
    row_size = lax.axis_size("row")
    query_low = w_query.astype(jnp.bfloat16)
    key_low = w_key.astype(jnp.bfloat16)
    value_low = w_value.astype(jnp.bfloat16)
    up_low = w_up.astype(jnp.bfloat16)
    out_low = w_out.astype(jnp.bfloat16)
    down_low = w_down.astype(jnp.bfloat16)
    query_full, key_full, value_full, up_full, out_full, down_full = (
        lax.all_gather(query_low, "row", axis=0, tiled=True),
        lax.all_gather(key_low, "row", axis=0, tiled=True),
        lax.all_gather(value_low, "row", axis=0, tiled=True),
        lax.all_gather(up_low, "row", axis=0, tiled=True),
        lax.all_gather(out_low, "row", axis=1, tiled=True),
        lax.all_gather(down_low, "row", axis=1, tiled=True),
    )
    step_onehot = (
        lax.broadcasted_iota(jnp.int32, (seq_count, table.shape[0]), 1) == timesteps[:, None]
    ).astype(jnp.float32)
    table_rows = jnp.dot(
        step_onehot, table, precision=lax.Precision.HIGHEST, preferred_element_type=jnp.float32
    )
    start = tokens.astype(jnp.float32) + table_rows[:, None, :]
    normed_one, unit_one, inverse_one = layer_norm_parts(start, gain_one, bias_one)
    rows_one = lax.all_gather(normed_one.astype(jnp.bfloat16), "col", axis=1, tiled=True).reshape(
        seq_count * full_len, model_width
    )
    query = (jnp.dot(rows_one, query_full, preferred_element_type=jnp.float32) + b_query).astype(
        jnp.bfloat16
    )
    key = jnp.dot(rows_one, key_full, preferred_element_type=jnp.float32).astype(jnp.bfloat16)
    value = (jnp.dot(rows_one, value_full, preferred_element_type=jnp.float32) + b_value).astype(
        jnp.bfloat16
    )
    query_seq = query.reshape(seq_count, block_count, row_block, local_heads, HEAD_DIM)
    key_seq = key.reshape(seq_count, full_len, local_heads, HEAD_DIM)
    value_seq = value.reshape(seq_count, full_len, local_heads, HEAD_DIM)
    query_ids_all = block_ids.reshape(seq_count, block_count, row_block)

    def scores_for(query_part, key_part, query_ids, key_ids):
        scores = (
            jnp.einsum("qhd,khd->hqk", query_part, key_part, preferred_element_type=jnp.float32)
            * scale_factor
        )
        allowed = key_ids[None, None, :] <= query_ids[None, :, None]
        return jnp.where(allowed, scores, masked_score)

    def forward_seq(pieces):
        query_blocks, key_part, value_part, ids_blocks, key_ids = pieces

        def forward_block(inner):
            query_part, query_ids = inner
            scores = scores_for(query_part, key_part, query_ids, key_ids)
            top = jnp.max(scores, axis=-1, keepdims=True)
            expo = jnp.exp(scores - top)
            total = jnp.sum(expo, axis=-1, keepdims=True)
            probs = (expo / total).astype(jnp.bfloat16)
            mixed = jnp.einsum(
                "hqk,khd->qhd", probs, value_part, preferred_element_type=jnp.float32
            )
            return (mixed, (top + jnp.log(total))[..., 0])

        return lax.map(forward_block, (query_blocks, ids_blocks))

    attended, log_sums = lax.map(
        forward_seq, (query_seq, key_seq, value_seq, query_ids_all, block_ids)
    )
    attended_low = attended.reshape(seq_count * full_len, head_cols).astype(jnp.bfloat16)
    branch_part = jnp.dot(attended_low, out_full, preferred_element_type=jnp.float32).reshape(
        seq_count, full_len, model_width
    )
    branch = lax.psum_scatter(branch_part, "col", scatter_dimension=1, tiled=True)
    middle = start + branch + b_out
    normed_two, unit_two, inverse_two = layer_norm_parts(middle, gain_two, bias_two)
    rows_two = lax.all_gather(normed_two.astype(jnp.bfloat16), "col", axis=1, tiled=True).reshape(
        seq_count * full_len, model_width
    )
    hidden_pre = jnp.dot(rows_two, up_full, preferred_element_type=jnp.float32) + b_up
    hidden_low = gelu_exact(hidden_pre).astype(jnp.bfloat16)
    mixer_part = jnp.dot(hidden_low, down_full, preferred_element_type=jnp.float32).reshape(
        seq_count, full_len, model_width
    )
    mixer = lax.psum_scatter(
        mixer_part.astype(jnp.bfloat16), "col", scatter_dimension=1, tiled=True
    ).astype(jnp.float32)
    layer_out = (middle + mixer + b_down).astype(jnp.bfloat16)
    grad_out = cotangent.astype(jnp.float32)
    grad_mixer_rows = lax.all_gather(cotangent, "col", axis=1, tiled=True).reshape(
        seq_count * full_len, model_width
    )
    grad_b_down = jnp.sum(cotangent, axis=(0, 1), dtype=jnp.float32)
    grad_down = jnp.einsum(
        "rf,rd->fd", hidden_low, grad_mixer_rows, preferred_element_type=jnp.float32
    )
    grad_hidden = jnp.einsum(
        "rd,fd->rf", grad_mixer_rows, down_full, preferred_element_type=jnp.float32
    )
    grad_pre = jax.vjp(gelu_exact, hidden_pre)[1](grad_hidden)[0]
    grad_pre_low = grad_pre.astype(jnp.bfloat16)
    grad_up = jnp.einsum("rd,rf->df", rows_two, grad_pre_low, preferred_element_type=jnp.float32)
    grad_b_up_local = jnp.sum(grad_pre_low, axis=0, dtype=jnp.float32)
    grad_normed_two_part = jnp.einsum(
        "rf,df->rd", grad_pre_low, up_full, preferred_element_type=jnp.float32
    ).reshape(seq_count, full_len, model_width)
    grad_normed_two = lax.psum_scatter(grad_normed_two_part, "col", scatter_dimension=1, tiled=True)
    grad_gain_two = jnp.sum(grad_normed_two * unit_two, axis=(0, 1))
    grad_bias_two = jnp.sum(grad_normed_two, axis=(0, 1))
    grad_middle = grad_out + norm_back(grad_normed_two, unit_two, inverse_two, gain_two)
    grad_branch_low = grad_middle.astype(jnp.bfloat16)
    grad_b_out = jnp.sum(grad_branch_low, axis=(0, 1), dtype=jnp.float32)
    grad_branch_rows = lax.all_gather(grad_branch_low, "col", axis=1, tiled=True).reshape(
        seq_count * full_len, model_width
    )
    grad_out_proj = jnp.einsum(
        "rh,rd->hd", attended_low, grad_branch_rows, preferred_element_type=jnp.float32
    )
    grad_attended = jnp.einsum(
        "rd,hd->rh", grad_branch_rows, out_full, preferred_element_type=jnp.float32
    ).astype(jnp.bfloat16)
    grad_att_seq = grad_attended.reshape(seq_count, block_count, row_block, local_heads, HEAD_DIM)

    def backward_seq(pieces):
        query_blocks, key_part, value_part, ids_blocks, key_ids, grad_blocks, sums_blocks = pieces

        def backward_block(carry, inner):
            query_part, query_ids, grad_part, log_part = inner
            scores = scores_for(query_part, key_part, query_ids, key_ids)
            probs = jnp.exp(scores - log_part[:, :, None])
            grad_probs = jnp.einsum(
                "qhd,khd->hqk", grad_part, value_part, preferred_element_type=jnp.float32
            )
            inner_sum = jnp.sum(probs * grad_probs, axis=-1, keepdims=True)
            grad_scores = (probs * (grad_probs - inner_sum)).astype(jnp.bfloat16)
            grad_query_part = (
                jnp.einsum(
                    "hqk,khd->qhd", grad_scores, key_part, preferred_element_type=jnp.float32
                )
                * scale_factor
            )
            key_acc = (
                carry[0]
                + jnp.einsum(
                    "hqk,qhd->khd", grad_scores, query_part, preferred_element_type=jnp.float32
                )
                * scale_factor
            )
            value_acc = carry[1] + jnp.einsum(
                "hqk,qhd->khd",
                probs.astype(jnp.bfloat16),
                grad_part,
                preferred_element_type=jnp.float32,
            )
            return ((key_acc, value_acc), grad_query_part)

        empty = jnp.zeros((full_len, local_heads, HEAD_DIM), jnp.float32)
        (grad_key_part, grad_value_part), grad_query_blocks = lax.scan(
            backward_block, (empty, empty), (query_blocks, ids_blocks, grad_blocks, sums_blocks)
        )
        return (grad_query_blocks, grad_key_part, grad_value_part)

    grad_query_all, grad_key_all, grad_value_all = lax.map(
        backward_seq,
        (query_seq, key_seq, value_seq, query_ids_all, block_ids, grad_att_seq, log_sums),
    )
    grad_query_low = grad_query_all.reshape(seq_count * full_len, head_cols).astype(jnp.bfloat16)
    grad_key_low = grad_key_all.reshape(seq_count * full_len, head_cols).astype(jnp.bfloat16)
    grad_value_low = grad_value_all.reshape(seq_count * full_len, head_cols).astype(jnp.bfloat16)
    grad_w_query = jnp.einsum(
        "rd,rh->dh", rows_one, grad_query_low, preferred_element_type=jnp.float32
    )
    grad_w_key = jnp.einsum("rd,rh->dh", rows_one, grad_key_low, preferred_element_type=jnp.float32)
    grad_w_value = jnp.einsum(
        "rd,rh->dh", rows_one, grad_value_low, preferred_element_type=jnp.float32
    )
    grad_b_query_local = jnp.sum(grad_query_low, axis=0, dtype=jnp.float32)
    grad_b_value_local = jnp.sum(grad_value_low, axis=0, dtype=jnp.float32)
    grad_normed_one_part = (
        jnp.einsum("rh,dh->rd", grad_query_low, query_full, preferred_element_type=jnp.float32)
        + jnp.einsum("rh,dh->rd", grad_key_low, key_full, preferred_element_type=jnp.float32)
        + jnp.einsum("rh,dh->rd", grad_value_low, value_full, preferred_element_type=jnp.float32)
    ).reshape(seq_count, full_len, model_width)
    grad_normed_one = lax.psum_scatter(grad_normed_one_part, "col", scatter_dimension=1, tiled=True)
    grad_gain_one = jnp.sum(grad_normed_one * unit_one, axis=(0, 1))
    grad_bias_one = jnp.sum(grad_normed_one, axis=(0, 1))
    grad_tokens = grad_middle + norm_back(grad_normed_one, unit_one, inverse_one, gain_one)
    token_sums = jnp.sum(grad_tokens, axis=1)

    def widen(local_vec, full_size):
        return lax.dynamic_update_slice_in_dim(
            jnp.zeros((full_size,), jnp.float32), local_vec, col_index * local_vec.shape[0], 0
        )

    wide_query_bias = widen(grad_b_query_local, model_width)
    wide_value_bias = widen(grad_b_value_local, model_width)
    wide_up_bias = widen(grad_b_up_local, hidden_cols * lax.axis_size("col"))
    grad_table = jnp.einsum(
        "sv,sd->vd",
        step_onehot,
        token_sums,
        precision=lax.Precision.HIGHEST,
        preferred_element_type=jnp.float32,
    )
    (
        sum_table,
        sum_gain_one,
        sum_bias_one,
        sum_query_bias,
        sum_value_bias,
        sum_out_bias,
        sum_gain_two,
        sum_bias_two,
        sum_up_bias,
        sum_down_bias,
    ) = lax.psum(
        (
            grad_table,
            grad_gain_one,
            grad_bias_one,
            wide_query_bias,
            wide_value_bias,
            grad_b_out,
            grad_gain_two,
            grad_bias_two,
            wide_up_bias,
            grad_b_down,
        ),
        ("dp", "row", "col"),
    )
    grad_b_query = lax.dynamic_slice_in_dim(sum_query_bias, col_index * head_cols, head_cols, 0)
    grad_b_value = lax.dynamic_slice_in_dim(sum_value_bias, col_index * head_cols, head_cols, 0)
    grad_b_up = lax.dynamic_slice_in_dim(sum_up_bias, col_index * hidden_cols, hidden_cols, 0)

    def owned_rows(grad_whole, dim_pick):
        share = grad_whole.shape[dim_pick] // row_size
        return lax.dynamic_slice_in_dim(grad_whole, row_index * share, share, dim_pick)

    summed = lax.psum(
        (grad_w_query, grad_w_key, grad_w_value, grad_up, grad_out_proj, grad_down), ("dp", "row")
    )
    owned_query = owned_rows(summed[0], 0)
    owned_key = owned_rows(summed[1], 0)
    owned_value = owned_rows(summed[2], 0)
    owned_up = owned_rows(summed[3], 0)
    owned_out = owned_rows(summed[4], 1)
    owned_down = owned_rows(summed[5], 1)
    return (
        layer_out,
        grad_tokens,
        sum_table,
        sum_gain_one,
        sum_bias_one,
        owned_query,
        owned_key,
        owned_value,
        grad_b_query,
        grad_b_value,
        owned_out,
        sum_out_bias,
        sum_gain_two,
        sum_bias_two,
        owned_up,
        grad_b_up,
        owned_down,
        sum_down_bias,
    )


def solution(mesh):
    return jax.shard_map(
        shards,
        mesh=mesh,
        in_specs=(
            P(("dp", "row"), "col", None),
            P(("dp", "row")),
            P(("dp", "row"), None),
            P(),
            P(),
            P(),
            P("row", "col"),
            P("row", "col"),
            P("row", "col"),
            P("col"),
            P("col"),
            P("col", "row"),
            P(),
            P(),
            P(),
            P("row", "col"),
            P("col"),
            P("col", "row"),
            P(),
            P(("dp", "row"), "col", None),
        ),
        out_specs=(
            P(("dp", "row"), "col", None),
            P(("dp", "row"), "col", None),
            P(),
            P(),
            P(),
            P("row", "col"),
            P("row", "col"),
            P("row", "col"),
            P("col"),
            P("col"),
            P("col", "row"),
            P(),
            P(),
            P(),
            P("row", "col"),
            P("col"),
            P("col", "row"),
            P(),
        ),
        check_vma=False,
    )
```

profile of v0, /device:TPU:0, one launch (start us, length us, event | category | flops | bytes accessed | tf_op | source)
XLA Modules:
  0.0 1383.5 jit_solution(9425003297407014153)
XLA Ops:
  81.4 149.2 %while.47 = (s32[]{:T(128)}, bf16[4,512,6,64]{1,3,2,0:T(8,128)(2,1)}, f32[4,6,512]{2,1,0:T(8,128)}, s32[2048]{0:T(1024)S(1)}, s32[4,512]{1,0:T(4,128)S(1)}, /*in...) while((s32[]{:T(128)}, ...), condition=%wide.region_5.6_spmd, body=%wide.region_2.5_spmd.sunk | while | flops 1687155712 | bytes 103016640 | solution.py:123
  242.2 12.7 reduce-scatter.5.cloned.1.call-done
  262.4 18.1 %all-gather.11.cloned.1.call-done = bf16[768,1536]{1,0:T(8,128)(2,1)} async-done(((bf16[192,1536]{1,0:T(8,128)(2,1)}), bf16[768,1536]{1,0:T(8,128)(2,1)}) %all-gather.11.cloned.1.call-update) | async-done | bytes 2359312 | tf_op jit(solution)/shard_map/all_gather | solution.py:73
  280.5 14.1 %all-gather.9.cloned.1.call-done = bf16[1,2048,768]{2,1,0:T(8,128)(2,1)} async-done(((bf16[1,1024,768]{2,1,0:T(8,128)(2,1)}), bf16[1,2048,768]{2,1,0:T(8,128)(2,1)}) %all-gather.9.cloned.1.call-update) | async-done | bytes 3145744 | tf_op jit(solution)/shard_map/all_gather | solution.py:135
  294.6 34.8 %multiply_convert_fusion.1 = (bf16[2048,1536]{1,0:T(8,128)(2,1)}, f32[2048,1536]{1,0:T(8,128)}, f32[2048,1536]{1,0:T(8,128)}) fusion(f32[1536]{0:T(1024)S(1)} %copy-done.70, bf16[768,1536]{1,0:T(8,128)(2,1)} %all-gather.11.cloned.1.call-done, bf16[1,2048,768]{2,1,0:T(8,128)(2,1)} %all-gather.9.cloned.1.call-done), kind=kOutput, calls=%fused_computation.51 | convolution fusion | flops 5039456256 | bytes 36968448 | tf_op jit(solution)/shard_map/dot_general | solution.py:138
  329.4 21.0 %all-gather.13.cloned.1.call-done = bf16[1536,768]{0,1:T(8,128)(2,1)} async-done(((bf16[1536,192]{0,1:T(8,128)(2,1)}), bf16[1536,768]{0,1:T(8,128)(2,1)}) %all-gather.13.cloned.1.call-update) | async-done | bytes 2359312 | tf_op jit(solution)/shard_map/all_gather | solution.py:75
  350.4 17.7 %convert_reduce_fusion = (f32[1536]{0:T(1024)}, bf16[2048,1536]{1,0:T(8,128)(2,1)S(1)}) fusion(f32[2048,1536]{1,0:T(8,128)} %get-tuple-element.325, bf16[1536,768]{0,1:T(8,128)(2,1)} %all-gather.13.cloned.1.call-done, bf16[1,2048,768]{2,1,0:T(8,128)(2,1)} %all-gather.15.cloned.1.call-done, f32[2048,1536]{1,0:T(8,128)} %get-tuple-element.334, ...), kind=kOutput, calls=%fused_computation.49 | convolution fusion | flops 4885314048 | bytes 36974592 | tf_op jit(solution)/shard_map/rd,fd->rf/dot_general | solution.py:155
  413.0 13.5 all-gather.17.cloned.1.call-done
  439.8 339.8 %while.48 = (s32[]{:T(128)}, f32[2048,6,64]{0,2,1:T(8,128)}, f32[2048,6,64]{0,2,1:T(8,128)}, bf16[4,512,6,64]{1,3,2,0:T(8,128)(2,1)}, bf16[4,512,6,64]{1,3,2,0:T...) while((s32[]{:T(128)}, f32[2048,6,64]{0,2,1:T(8,128)}, ...), condition=%wide.region_15.16_spmd.clone, body=%wide.region_13.15_spmd.clone.sunk | while | flops 4126077952 | bytes 212699312 | solution.py:216
  453.5 12.9 bitcast_add_fusion.5
  466.4 18.1 %multiply_reduce_fusion.10 = (f32[6,512]{1,0:T(8,128)S(1)}, f32[6,512,2048]{2,1,0:T(8,128)}) fusion(f32[6,512,2048]{2,1,0:T(8,128)} %fusion.147, f32[6,512]{1,0:T(8,128)S(1)} %dynamic-slice_bitcast_fusion.2, pred[512,2048]{1,0:T(8,128)(4,1)S(1)} %broadcast_compare_fusion.5, bf16[2048,6,64]{0,2,1:T(8,128)(2,1)} %get-tuple-element.526, ...), kind=kOutput, calls=%fused_computation.18.clone.1 | convolution fusion | flops 836760576 | bytes 53370884 | tf_op jit(solution)/shard_map/while/body/eval_jaxpr/while/body/eval_jaxpr/qhd,khd->hqk/dot_general | solution.py:189
  484.5 21.3 %multiply_convert_fusion.3 = bf16[6,512,2048]{2,1,0:T(8,128)(2,1)} fusion(f32[6,512,2048]{2,1,0:T(8,128)} %get-tuple-element.461, f32[6,512,2048]{2,1,0:T(8,128)} %fusion.147, f32[6,512]{1,0:T(8,128)S(1)} %get-tuple-element.462, f32[6,512]{1,0:T(8,128)S(1)} %dynamic-slice_bitcast_fusion.2, pred[512,2048]{1,0:T(8,128)(4,1)S(1)} %broadcast_compare_fusion.5), kind=kLoop, calls=%fused_computation.17.clone.1 | loop fusion | flops 37748736 | bytes 63987712 | tf_op jit(solution)/shard_map/while/body/eval_jaxpr/while/body/eval_jaxpr/convert_element_type | solution.py:193
  536.9 13.8 bitcast_add_fusion.5
  550.7 18.1 %multiply_reduce_fusion.10 = (f32[6,512]{1,0:T(8,128)S(1)}, f32[6,512,2048]{2,1,0:T(8,128)}) fusion(f32[6,512,2048]{2,1,0:T(8,128)} %fusion.147, f32[6,512]{1,0:T(8,128)S(1)} %dynamic-slice_bitcast_fusion.2, pred[512,2048]{1,0:T(8,128)(4,1)S(1)} %broadcast_compare_fusion.5, bf16[2048,6,64]{0,2,1:T(8,128)(2,1)} %get-tuple-element.526, ...), kind=kOutput, calls=%fused_computation.18.clone.1 | convolution fusion | flops 836760576 | bytes 53370884 | tf_op jit(solution)/shard_map/while/body/eval_jaxpr/while/body/eval_jaxpr/qhd,khd->hqk/dot_general | solution.py:189
  568.8 21.3 %multiply_convert_fusion.3 = bf16[6,512,2048]{2,1,0:T(8,128)(2,1)} fusion(f32[6,512,2048]{2,1,0:T(8,128)} %get-tuple-element.461, f32[6,512,2048]{2,1,0:T(8,128)} %fusion.147, f32[6,512]{1,0:T(8,128)S(1)} %get-tuple-element.462, f32[6,512]{1,0:T(8,128)S(1)} %dynamic-slice_bitcast_fusion.2, pred[512,2048]{1,0:T(8,128)(4,1)S(1)} %broadcast_compare_fusion.5), kind=kLoop, calls=%fused_computation.17.clone.1 | loop fusion | flops 37748736 | bytes 63987712 | tf_op jit(solution)/shard_map/while/body/eval_jaxpr/while/body/eval_jaxpr/convert_element_type | solution.py:193
  622.2 13.8 bitcast_add_fusion.5
  636.0 18.1 %multiply_reduce_fusion.10 = (f32[6,512]{1,0:T(8,128)S(1)}, f32[6,512,2048]{2,1,0:T(8,128)}) fusion(f32[6,512,2048]{2,1,0:T(8,128)} %fusion.147, f32[6,512]{1,0:T(8,128)S(1)} %dynamic-slice_bitcast_fusion.2, pred[512,2048]{1,0:T(8,128)(4,1)S(1)} %broadcast_compare_fusion.5, bf16[2048,6,64]{0,2,1:T(8,128)(2,1)} %get-tuple-element.526, ...), kind=kOutput, calls=%fused_computation.18.clone.1 | convolution fusion | flops 836760576 | bytes 53370884 | tf_op jit(solution)/shard_map/while/body/eval_jaxpr/while/body/eval_jaxpr/qhd,khd->hqk/dot_general | solution.py:189
  654.1 21.3 %multiply_convert_fusion.3 = bf16[6,512,2048]{2,1,0:T(8,128)(2,1)} fusion(f32[6,512,2048]{2,1,0:T(8,128)} %get-tuple-element.461, f32[6,512,2048]{2,1,0:T(8,128)} %fusion.147, f32[6,512]{1,0:T(8,128)S(1)} %get-tuple-element.462, f32[6,512]{1,0:T(8,128)S(1)} %dynamic-slice_bitcast_fusion.2, pred[512,2048]{1,0:T(8,128)(4,1)S(1)} %broadcast_compare_fusion.5), kind=kLoop, calls=%fused_computation.17.clone.1 | loop fusion | flops 37748736 | bytes 63987712 | tf_op jit(solution)/shard_map/while/body/eval_jaxpr/while/body/eval_jaxpr/convert_element_type | solution.py:193
  707.5 13.8 bitcast_add_fusion.5
  721.3 18.1 %multiply_reduce_fusion.10 = (f32[6,512]{1,0:T(8,128)S(1)}, f32[6,512,2048]{2,1,0:T(8,128)}) fusion(f32[6,512,2048]{2,1,0:T(8,128)} %fusion.147, f32[6,512]{1,0:T(8,128)S(1)} %dynamic-slice_bitcast_fusion.2, pred[512,2048]{1,0:T(8,128)(4,1)S(1)} %broadcast_compare_fusion.5, bf16[2048,6,64]{0,2,1:T(8,128)(2,1)} %get-tuple-element.526, ...), kind=kOutput, calls=%fused_computation.18.clone.1 | convolution fusion | flops 836760576 | bytes 53370884 | tf_op jit(solution)/shard_map/while/body/eval_jaxpr/while/body/eval_jaxpr/qhd,khd->hqk/dot_general | solution.py:189
  739.4 21.3 %multiply_convert_fusion.3 = bf16[6,512,2048]{2,1,0:T(8,128)(2,1)} fusion(f32[6,512,2048]{2,1,0:T(8,128)} %get-tuple-element.461, f32[6,512,2048]{2,1,0:T(8,128)} %fusion.147, f32[6,512]{1,0:T(8,128)S(1)} %get-tuple-element.462, f32[6,512]{1,0:T(8,128)S(1)} %dynamic-slice_bitcast_fusion.2, pred[512,2048]{1,0:T(8,128)(4,1)S(1)} %broadcast_compare_fusion.5), kind=kLoop, calls=%fused_computation.17.clone.1 | loop fusion | flops 37748736 | bytes 63987712 | tf_op jit(solution)/shard_map/while/body/eval_jaxpr/while/body/eval_jaxpr/convert_element_type | solution.py:193
  839.1 46.3 %all-reduce = (f32[768]{0:T(1024)}, f32[768]{0:T(1024)}, f32[768]{0:T(1024)S(1)}, f32[768]{0:T(1024)S(1)}, f32[768]{0:T(1024)}, /*index=5*/f32[768]{0:T(1024)}, f32[768]{0:T(1024)}, f32[3072]{0:T(1024)S(1)}, f32[768]{0:T(1024)}) all-reduce(f32[768]{0:T(1024)S(1)} %get-tuple-element.258, ...), channel_id=1, replica_groups=mesh['dp'=4,'row'=4,'col'=2] {'dp','row','col'}, use_global_device_ids=true, to_apply=%region_22.23 | all-reduce | flops 9216 | bytes 73728 | tf_op jit(solution)/shard_map/psum | solution.py:274
  887.4 341.9 %all-reduce.7.cloned.1.call-done = (f32[768,384]{1,0:T(8,128)}, f32[768,384]{1,0:T(8,128)}, f32[768,384]{1,0:T(8,128)}, f32[384,768]{0,1:T(8,128)}, f32[768,1536]{1,0:T(8,128)}, /*index=5*/f32[1536,768]{0,1:T(8,128)}) async-done(((f32[768,384]{1,0:T(8,128)}, f32[768,384]{1,0:T(8,128)}, f32[768,384]{1,0:T(8,128)}, f32[384,768]{0,1:T(8,128)}, f32[768,1536]{1,0:T(8,128)}, /*index=5*/f32[1536,768]{0,1:T(8,128)}), ...) | async-done | bytes 14155792 | tf_op jit(solution)/shard_map/psum | solution.py:297
  1240.9 131.2 %all-reduce.5.cloned.1.call-done = f32[1000,768]{1,0:T(8,128)} async-done(((f32[1000,768]{1,0:T(8,128)}), f32[1000,768]{1,0:T(8,128)}) %all-reduce.5.cloned.1.call-update) | async-done | bytes 3072016 | tf_op jit(solution)/shard_map/psum | solution.py:274
  (330 shorter events, 501.7 us)
Async XLA Ops:
  8.1 52.9 %all-gather.7.cloned.1.call-start = ((), (), s32[]{:S(2)}) async-start(), calls=%async_computation.4 | async-start | bytes 4718592 | tf_op jit(solution)/shard_map/all_gather | solution.py:85
  14.6 47.2 %copy-start.71 = (f32[384]{0:T(512)S(1)}, f32[384]{0:T(512)}, u32[]{:S(2)}) copy-start(f32[384]{0:T(512)} %param.33) | copy-start | bytes 4612
  14.6 240.3 %reduce-scatter.5.cloned.1.call-start = ((), (), s32[]{:S(2)}) async-start(), calls=%async_computation.5 | async-start | bytes 9437184 | tf_op jit(solution)/shard_map/reduce_scatter | solution.py:132
  93.7 12.1 copy-start.20
  130.9 12.1 copy-start.20
  239.9 14.9 %copy-start.6 = (bf16[1,1024,768]{2,1,0:T(8,128)(2,1)S(1)}, bf16[1,1024,768]{2,1,0:T(8,128)(2,1)}, u32[]{:S(2)}) copy-start(bf16[1,1024,768]{2,1,0:T(8,128)(2,1)} %param.24) | copy-start | bytes 4718596
  239.9 14.9 %copy-start.40 = (f32[768]{0:T(1024)S(1)}, f32[768]{0:T(1024)}, u32[]{:S(2)}) copy-start(f32[768]{0:T(1024)} %copy-done.39) | copy-start | bytes 9220
  239.9 14.9 %copy-start.61 = (f32[768]{0:T(1024)S(1)}, f32[768]{0:T(1024)}, u32[]{:S(2)}) copy-start(f32[768]{0:T(1024)} %param.36) | copy-start | bytes 9220
  240.0 40.5 %all-gather.11.cloned.1.call-start = ((), (), s32[]{:S(2)}) async-start(), calls=%async_computation.7 | async-start | bytes 2949120 | tf_op jit(solution)/shard_map/all_gather | solution.py:73
  242.1 52.5 %all-gather.9.cloned.1.call-start = ((), (), s32[]{:S(2)}) async-start(), calls=%async_computation.6 | async-start | bytes 4718592 | tf_op jit(solution)/shard_map/all_gather | solution.py:135
  260.7 33.8 %copy-start.70 = (f32[1536]{0:T(1024)S(1)}, f32[1536]{0:T(1024)}, u32[]{:S(2)}) copy-start(f32[1536]{0:T(1024)} %param.40) | copy-start | bytes 18436
  260.8 68.6 %all-gather.15.cloned.1.call-start = ((), (), s32[]{:S(2)}) async-start(), calls=%async_computation.10 | async-start | bytes 4718592 | tf_op jit(solution)/shard_map/all_gather | solution.py:148
  261.4 89.0 %all-gather.13.cloned.1.call-start = ((), (), s32[]{:S(2)}) async-start(), calls=%async_computation.8 | async-start | bytes 2949120 | tf_op jit(solution)/shard_map/all_gather | solution.py:75
  262.3 129.9 %reduce-scatter.9.cloned.1.call-start = ((), (), s32[]{:S(2)}) async-start(), calls=%async_computation.11 | async-start | bytes 9437184 | tf_op jit(solution)/shard_map/reduce_scatter | solution.py:165
  350.4 20.3 %copy-start.68 = (bf16[768,1536]{1,0:T(8,128)(2,1)S(1)}, bf16[768,1536]{1,0:T(8,128)(2,1)}, u32[]{:S(2)}) copy-start(bf16[768,1536]{1,0:T(8,128)(2,1)} %all-gather.11.cloned.1.call-done) | copy-start | bytes 7077892
  377.7 28.7 %reduce-scatter.7.cloned.1.call-start = ((), (), s32[]{:S(2)}) async-start(), calls=%async_computation.9 | async-start | bytes 4718592 | tf_op jit(solution)/shard_map/reduce_scatter | solution.py:143
  388.8 17.7 %copy-start.22 = (bf16[1,1024,768]{2,1,0:T(8,128)(2,1)S(1)}, bf16[1,1024,768]{2,1,0:T(8,128)(2,1)}, u32[]{:S(2)}) copy-start(bf16[1,1024,768]{2,1,0:T(8,128)(2,1)} %param.43) | copy-start | bytes 4718596
  388.8 17.6 %copy-start.63 = (f32[768]{0:T(1024)S(1)}, f32[768]{0:T(1024)}, u32[]{:S(2)}) copy-start(f32[768]{0:T(1024)} %param.42) | copy-start | bytes 9220
  388.9 37.6 %all-gather.17.cloned.1.call-start = ((), (), s32[]{:S(2)}) async-start(), calls=%async_computation.12 | async-start | bytes 4718592 | tf_op jit(solution)/shard_map/all_gather | solution.py:171
  406.5 20.0 %copy-start.30 = (bf16[384,768]{0,1:T(8,128)(2,1)S(1)}, bf16[384,768]{0,1:T(8,128)(2,1)}, u32[]{:S(2)}) copy-start(bf16[384,768]{0,1:T(8,128)(2,1)} %all_gather.34) | copy-start | bytes 1769476
  413.0 414.2 %reduce-scatter.11.cloned.1.call-start = ((), (), s32[]{:S(2)}) async-start(), calls=%async_computation.13 | async-start | bytes 9437184 | tf_op jit(solution)/shard_map/reduce_scatter | solution.py:242
  794.7 434.6 %all-reduce.7.cloned.1.call-start = ((), (), s32[]{:S(2)}) async-start(), calls=%async_computation.15 | async-start | bytes 28311552 | tf_op jit(solution)/shard_map/psum | solution.py:297
  827.1 545.0 %all-reduce.5.cloned.1.call-start = ((), (), s32[]{:S(2)}) async-start(), calls=%async_computation.14 | async-start | bytes 6144000 | tf_op jit(solution)/shard_map/psum | solution.py:274
  1238.4 137.4 %copy-start.1 = (f32[1000,768]{1,0:T(8,128)S(1)}, f32[1000,768]{1,0:T(8,128)}, u32[]{:S(2)}) copy-start(f32[1000,768]{1,0:T(8,128)} %param.27) | copy-start | bytes 9216004
  (71 other events, 266.5 us)
Sparse Core Ops, SparseCore 0:
  14.7 14.8 all-gather.6
  240.1 14.7 reduce-scatter.4
  413.1 13.3 all-gather.16
  794.8 15.6 reduce-scatter.10
  827.2 402.0 all-reduce.6
  1236.1 135.9 all-reduce.4
Sparse Core Ops, SparseCore 1:
  242.9 37.5 all-gather.10
  282.5 12.0 all-gather.8
  296.0 13.2 all-gather.14
  311.9 38.5 all-gather.12
  377.8 14.3 reduce-scatter.8
  394.5 12.0 reduce-scatter.6
where the time goes:
time: 1390 us; the launch traced here: 1380 us
  waiting for transfers between devices  567 us (41%)
  matrix products  470 us (34%)
  other arithmetic  177 us (13%)
  blocking collectives  91.2 us (7%)
  local copies, waits for them, and re-layouts  60.1 us (4%)
  between operations  17.5 us (1%)
    psum x1, waiting for transfers between devices, shards(): lax.psum((grad_w_query, grad_w_key, grad_w_value, grad_up, grad_out_proj,...  342 us
    psum x1, waiting for transfers between devices, shards(): lax.psum((grad_table, grad_gain_one, grad_bias_one, wide_query_bias, wide...  131 us
    dot_general x8, matrix products, scores_for(): jnp.einsum('qhd,khd->hqk', query_part, key_part, preferred_element_type=j...  91.3 us
    convert_element_type x4, other arithmetic, backward_block(): grad_scores = (probs * (grad_probs - inner_sum)).astype(jnp.bfloat16)  85 us
    dot_general x4, matrix products, backward_block(): jnp.einsum('qhd,khd->hqk', grad_part, value_part, preferred_element_type=...  72.5 us
    dot_general x4, matrix products, backward_block(): jnp.einsum('hqk,qhd->khd', probs.astype(jnp.bfloat16), grad_part, preferr...  54.3 us
    reduce_sum x4, other arithmetic, forward_block(): total = jnp.sum(expo, axis=-1, keepdims=True)  48.3 us
    dot_general x4, matrix products, forward_block(): jnp.einsum('hqk,khd->qhd', probs, value_part, preferred_element_type=jnp....  46.5 us
  transfers between devices with their start and end apart: 12, of which 9 were waited for; matrix products, arithmetic and copies ran while one was open for 8% of the time, Pallas kernels for 0%

commit v1 on v0

--- a/solution.py
+++ b/solution.py
@@ -260,6 +260,9 @@
         precision=lax.Precision.HIGHEST,
         preferred_element_type=jnp.float32,
     )
+    _prepare_sizes = lambda net_axis, array_here, link_axis: lax.psum(
+        lax.psum(array_here, axis_name=link_axis), axis_name=net_axis
+    )
     (
         sum_table,
         sum_gain_one,
@@ -271,7 +274,8 @@
         sum_bias_two,
         sum_up_bias,
         sum_down_bias,
-    ) = lax.psum(
+    ) = _prepare_sizes(
+        "dp",
         (
             grad_table,
             grad_gain_one,
@@ -284,7 +288,7 @@
             wide_up_bias,
             grad_b_down,
         ),
-        ("dp", "row", "col"),
+        ("row", "col"),
     )
     grad_b_query = lax.dynamic_slice_in_dim(sum_query_bias, col_index * head_cols, head_cols, 0)
     grad_b_value = lax.dynamic_slice_in_dim(sum_value_bias, col_index * head_cols, head_cols, 0)

time: 1390 us -> 1440 us (1.036)
  waiting for transfers between devices: 567 us -> 616 us
    psum x1 -> x2, waiting for transfers between devices: 131 us -> 165 us  [the longest x1 108 us: shards(): lax.psum(lax.psum(array_here, axis_name=link_axis), axis_name=net_axis)]
    psum x1, waiting for transfers between devices: 342 us -> 358 us  [shards(): lax.psum((grad_w_query, grad_w_key, grad_w_value, grad_up, grad_out_proj,...]
    psum x1 -> x2, blocking collectives: 46.3 us -> 47.3 us  [the longest x1 24.9 us: shards(): lax.psum(array_here, axis_name=link_axis)]
  transfers between devices with their start and end apart: 12 -> 13, of which waited for: 9 -> 10; matrix products, arithmetic and copies ran while one was open for 8% -> 7% of each run, Pallas kernels for 0% -> 0%
where the time goes in v1:
time: 1440 us; the launch traced here: 1430 us
  waiting for transfers between devices  616 us (43%)
  matrix products  471 us (33%)
  other arithmetic  176 us (12%)
  blocking collectives  92.3 us (6%)
  local copies, waits for them, and re-layouts  59 us (4%)
  between operations  17.6 us (1%)
    psum x1, waiting for transfers between devices, shards(): lax.psum((grad_w_query, grad_w_key, grad_w_value, grad_up, grad_out_proj,...  358 us
    psum x1, waiting for transfers between devices, shards(): lax.psum(lax.psum(array_here, axis_name=link_axis), axis_name=net_axis)  108 us
    dot_general x8, matrix products, scores_for(): jnp.einsum('qhd,khd->hqk', query_part, key_part, preferred_element_type=j...  90.5 us
    convert_element_type x4, other arithmetic, backward_block(): grad_scores = (probs * (grad_probs - inner_sum)).astype(jnp.bfloat16)  84.9 us
    dot_general x4, matrix products, backward_block(): jnp.einsum('qhd,khd->hqk', grad_part, value_part, preferred_element_type=...  72.5 us
    psum x1, waiting for transfers between devices, shards(): lax.psum(array_here, axis_name=link_axis)  56.4 us
    dot_general x4, matrix products, backward_block(): jnp.einsum('hqk,qhd->khd', probs.astype(jnp.bfloat16), grad_part, preferr...  53.9 us
    reduce_sum x4, other arithmetic, forward_block(): total = jnp.sum(expo, axis=-1, keepdims=True)  48.3 us
  transfers between devices with their start and end apart: 13, of which 10 were waited for; matrix products, arithmetic and copies ran while one was open for 7% of the time, Pallas kernels for 0%

profile of v1, /device:TPU:0, one launch (start us, length us, event | category | flops | bytes accessed | tf_op | source)
XLA Modules:
  0.0 1434.1 jit_solution(9562234132266401281)
XLA Ops:
  81.4 148.8 %while.47 = (s32[]{:T(128)}, bf16[4,512,6,64]{1,3,2,0:T(8,128)(2,1)}, f32[4,6,512]{2,1,0:T(8,128)}, s32[2048]{0:T(1024)S(1)}, s32[4,512]{1,0:T(4,128)S(1)}, /*in...) while((s32[]{:T(128)}, ...), condition=%wide.region_5.6_spmd, body=%wide.region_2.5_spmd.sunk | while | flops 1687155712 | bytes 103016640 | solution.py:123
  262.0 18.1 %all-gather.11.cloned.1.call-done = bf16[768,1536]{1,0:T(8,128)(2,1)} async-done(((bf16[192,1536]{1,0:T(8,128)(2,1)}), bf16[768,1536]{1,0:T(8,128)(2,1)}) %all-gather.11.cloned.1.call-update) | async-done | bytes 2359312 | tf_op jit(solution)/shard_map/all_gather | solution.py:73
  280.0 14.1 all-gather.9.cloned.1.call-done
  294.1 34.8 %multiply_convert_fusion.1 = (bf16[2048,1536]{1,0:T(8,128)(2,1)}, f32[2048,1536]{1,0:T(8,128)}, f32[2048,1536]{1,0:T(8,128)}) fusion(f32[1536]{0:T(1024)S(1)} %copy-done.69, bf16[768,1536]{1,0:T(8,128)(2,1)} %all-gather.11.cloned.1.call-done, bf16[1,2048,768]{2,1,0:T(8,128)(2,1)} %all-gather.9.cloned.1.call-done), kind=kOutput, calls=%fused_computation.51 | convolution fusion | flops 5039456256 | bytes 36968448 | tf_op jit(solution)/shard_map/dot_general | solution.py:138
  329.0 21.0 %all-gather.13.cloned.1.call-done = bf16[1536,768]{0,1:T(8,128)(2,1)} async-done(((bf16[1536,192]{0,1:T(8,128)(2,1)}), bf16[1536,768]{0,1:T(8,128)(2,1)}) %all-gather.13.cloned.1.call-update) | async-done | bytes 2359312 | tf_op jit(solution)/shard_map/all_gather | solution.py:75
  350.0 17.7 %convert_reduce_fusion = (f32[1536]{0:T(1024)}, bf16[2048,1536]{1,0:T(8,128)(2,1)S(1)}) fusion(f32[2048,1536]{1,0:T(8,128)} %get-tuple-element.334, bf16[1536,768]{0,1:T(8,128)(2,1)} %all-gather.13.cloned.1.call-done, bf16[1,2048,768]{2,1,0:T(8,128)(2,1)} %all-gather.15.cloned.1.call-done, f32[2048,1536]{1,0:T(8,128)} %get-tuple-element.343, ...), kind=kOutput, calls=%fused_computation.49 | convolution fusion | flops 4885314048 | bytes 36974592 | tf_op jit(solution)/shard_map/rd,fd->rf/dot_general | solution.py:155
  412.6 13.5 all-gather.17.cloned.1.call-done
  439.4 338.9 %while.48 = (s32[]{:T(128)}, f32[2048,6,64]{0,2,1:T(8,128)}, f32[2048,6,64]{0,2,1:T(8,128)}, bf16[4,512,6,64]{1,3,2,0:T(8,128)(2,1)}, bf16[4,512,6,64]{1,3,2,0:T...) while((s32[]{:T(128)}, f32[2048,6,64]{0,2,1:T(8,128)}, ...), condition=%wide.region_15.16_spmd.clone, body=%wide.region_13.15_spmd.clone.sunk | while | flops 4126077952 | bytes 212699312 | solution.py:216
  465.8 18.1 %multiply_reduce_fusion.10 = (f32[6,512]{1,0:T(8,128)S(1)}, f32[6,512,2048]{2,1,0:T(8,128)}) fusion(f32[6,512,2048]{2,1,0:T(8,128)} %fusion.147, f32[6,512]{1,0:T(8,128)S(1)} %dynamic-slice_bitcast_fusion.2, pred[512,2048]{1,0:T(8,128)(4,1)S(1)} %broadcast_compare_fusion.5, bf16[2048,6,64]{0,2,1:T(8,128)(2,1)} %get-tuple-element.535, ...), kind=kOutput, calls=%fused_computation.18.clone.1 | convolution fusion | flops 836760576 | bytes 53370884 | tf_op jit(solution)/shard_map/while/body/eval_jaxpr/while/body/eval_jaxpr/qhd,khd->hqk/dot_general | solution.py:189
  483.9 21.2 %multiply_convert_fusion.3 = bf16[6,512,2048]{2,1,0:T(8,128)(2,1)} fusion(f32[6,512,2048]{2,1,0:T(8,128)} %get-tuple-element.470, f32[6,512,2048]{2,1,0:T(8,128)} %fusion.147, f32[6,512]{1,0:T(8,128)S(1)} %get-tuple-element.471, f32[6,512]{1,0:T(8,128)S(1)} %dynamic-slice_bitcast_fusion.2, pred[512,2048]{1,0:T(8,128)(4,1)S(1)} %broadcast_compare_fusion.5), kind=kLoop, calls=%fused_computation.17.clone.1 | loop fusion | flops 37748736 | bytes 63987712 | tf_op jit(solution)/shard_map/while/body/eval_jaxpr/while/body/eval_jaxpr/convert_element_type | solution.py:193
  536.2 13.7 bitcast_add_fusion.5
  549.9 18.1 %multiply_reduce_fusion.10 = (f32[6,512]{1,0:T(8,128)S(1)}, f32[6,512,2048]{2,1,0:T(8,128)}) fusion(f32[6,512,2048]{2,1,0:T(8,128)} %fusion.147, f32[6,512]{1,0:T(8,128)S(1)} %dynamic-slice_bitcast_fusion.2, pred[512,2048]{1,0:T(8,128)(4,1)S(1)} %broadcast_compare_fusion.5, bf16[2048,6,64]{0,2,1:T(8,128)(2,1)} %get-tuple-element.535, ...), kind=kOutput, calls=%fused_computation.18.clone.1 | convolution fusion | flops 836760576 | bytes 53370884 | tf_op jit(solution)/shard_map/while/body/eval_jaxpr/while/body/eval_jaxpr/qhd,khd->hqk/dot_general | solution.py:189
  568.0 21.2 %multiply_convert_fusion.3 = bf16[6,512,2048]{2,1,0:T(8,128)(2,1)} fusion(f32[6,512,2048]{2,1,0:T(8,128)} %get-tuple-element.470, f32[6,512,2048]{2,1,0:T(8,128)} %fusion.147, f32[6,512]{1,0:T(8,128)S(1)} %get-tuple-element.471, f32[6,512]{1,0:T(8,128)S(1)} %dynamic-slice_bitcast_fusion.2, pred[512,2048]{1,0:T(8,128)(4,1)S(1)} %broadcast_compare_fusion.5), kind=kLoop, calls=%fused_computation.17.clone.1 | loop fusion | flops 37748736 | bytes 63987712 | tf_op jit(solution)/shard_map/while/body/eval_jaxpr/while/body/eval_jaxpr/convert_element_type | solution.py:193
  621.2 13.7 bitcast_add_fusion.5
  634.9 18.1 %multiply_reduce_fusion.10 = (f32[6,512]{1,0:T(8,128)S(1)}, f32[6,512,2048]{2,1,0:T(8,128)}) fusion(f32[6,512,2048]{2,1,0:T(8,128)} %fusion.147, f32[6,512]{1,0:T(8,128)S(1)} %dynamic-slice_bitcast_fusion.2, pred[512,2048]{1,0:T(8,128)(4,1)S(1)} %broadcast_compare_fusion.5, bf16[2048,6,64]{0,2,1:T(8,128)(2,1)} %get-tuple-element.535, ...), kind=kOutput, calls=%fused_computation.18.clone.1 | convolution fusion | flops 836760576 | bytes 53370884 | tf_op jit(solution)/shard_map/while/body/eval_jaxpr/while/body/eval_jaxpr/qhd,khd->hqk/dot_general | solution.py:189
  653.0 21.2 %multiply_convert_fusion.3 = bf16[6,512,2048]{2,1,0:T(8,128)(2,1)} fusion(f32[6,512,2048]{2,1,0:T(8,128)} %get-tuple-element.470, f32[6,512,2048]{2,1,0:T(8,128)} %fusion.147, f32[6,512]{1,0:T(8,128)S(1)} %get-tuple-element.471, f32[6,512]{1,0:T(8,128)S(1)} %dynamic-slice_bitcast_fusion.2, pred[512,2048]{1,0:T(8,128)(4,1)S(1)} %broadcast_compare_fusion.5), kind=kLoop, calls=%fused_computation.17.clone.1 | loop fusion | flops 37748736 | bytes 63987712 | tf_op jit(solution)/shard_map/while/body/eval_jaxpr/while/body/eval_jaxpr/convert_element_type | solution.py:193
  706.3 13.7 bitcast_add_fusion.5
  720.0 18.1 %multiply_reduce_fusion.10 = (f32[6,512]{1,0:T(8,128)S(1)}, f32[6,512,2048]{2,1,0:T(8,128)}) fusion(f32[6,512,2048]{2,1,0:T(8,128)} %fusion.147, f32[6,512]{1,0:T(8,128)S(1)} %dynamic-slice_bitcast_fusion.2, pred[512,2048]{1,0:T(8,128)(4,1)S(1)} %broadcast_compare_fusion.5, bf16[2048,6,64]{0,2,1:T(8,128)(2,1)} %get-tuple-element.535, ...), kind=kOutput, calls=%fused_computation.18.clone.1 | convolution fusion | flops 836760576 | bytes 53370884 | tf_op jit(solution)/shard_map/while/body/eval_jaxpr/while/body/eval_jaxpr/qhd,khd->hqk/dot_general | solution.py:189
  738.1 21.2 %multiply_convert_fusion.3 = bf16[6,512,2048]{2,1,0:T(8,128)(2,1)} fusion(f32[6,512,2048]{2,1,0:T(8,128)} %get-tuple-element.470, f32[6,512,2048]{2,1,0:T(8,128)} %fusion.147, f32[6,512]{1,0:T(8,128)S(1)} %get-tuple-element.471, f32[6,512]{1,0:T(8,128)S(1)} %dynamic-slice_bitcast_fusion.2, pred[512,2048]{1,0:T(8,128)(4,1)S(1)} %broadcast_compare_fusion.5), kind=kLoop, calls=%fused_computation.17.clone.1 | loop fusion | flops 37748736 | bytes 63987712 | tf_op jit(solution)/shard_map/while/body/eval_jaxpr/while/body/eval_jaxpr/convert_element_type | solution.py:193
  837.4 56.4 %all-reduce.7.cloned.1.call-done = f32[1000,768]{1,0:T(8,128)} async-done(((f32[1000,768]{1,0:T(8,128)}), f32[1000,768]{1,0:T(8,128)}) %all-reduce.7.cloned.1.call-update) | async-done | bytes 3072016 | tf_op jit(solution)/shard_map/psum | solution.py:264
  895.0 24.9 %all-reduce.1 = (f32[768]{0:T(1024)S(1)}, f32[768]{0:T(1024)S(1)}, f32[768]{0:T(1024)S(1)}, f32[768]{0:T(1024)S(1)}, f32[768]{0:T(1024)S(1)}, /*index=5*/f32[768...) all-reduce(f32[768]{0:T(1024)S(1)} %get-tuple-element.258, ...), channel_id=1, replica_groups=mesh['dp'=4,'row'=4,'col'=2] {'row','col'}, use_global_device_ids=true, to_apply=%region_23.24 | all-reduce | flops 9216 | bytes 73728 | tf_op jit(solution)/shard_map/psum | solution.py:264
  920.0 22.4 %all-reduce.2 = (f32[768]{0:T(1024)}, f32[768]{0:T(1024)}, f32[768]{0:T(1024)S(1)}, f32[768]{0:T(1024)S(1)}, f32[768]{0:T(1024)}, /*index=5*/f32[768]{0:T(1024)}...) all-reduce(f32[768]{0:T(1024)S(1)} %get-tuple-element.308, ...), channel_id=1, replica_groups=mesh['dp'=4,'row'=4,'col'=2] {'dp'}, use_global_device_ids=true, to_apply=%region_24.25 | all-reduce | flops 9216 | bytes 73728 | tf_op jit(solution)/shard_map/psum | solution.py:263
  944.3 358.1 %all-reduce.11.cloned.1.call-done = (f32[768,384]{1,0:T(8,128)}, f32[768,384]{1,0:T(8,128)}, f32[768,384]{1,0:T(8,128)}, f32[384,768]{0,1:T(8,128)}, f32[768,1536]{1,0:T(8,128)}, /*index=5*/f32[1536,768]{0,1:T(8,128)}) async-done(((f32[768,384]{1,0:T(8,128)}, f32[768,384]{1,0:T(8,128)}, f32[768,384]{1,0:T(8,128)}, f32[384,768]{0,1:T(8,128)}, f32[768,1536]{1,0:T(8,128)}, /*index=5*/f32[1536,768]{0,1:T(8,128)}), ...) | async-done | bytes 14155792 | tf_op jit(solution)/shard_map/psum | solution.py:301
  1314.2 108.5 %all-reduce.9.cloned.1.call-done = f32[1000,768]{1,0:T(8,128)} async-done(((f32[1000,768]{1,0:T(8,128)}), f32[1000,768]{1,0:T(8,128)}) %all-reduce.9.cloned.1.call-update) | async-done | bytes 3072016 | tf_op jit(solution)/shard_map/psum | solution.py:263
  (332 shorter events, 527.3 us)
Async XLA Ops:
  8.1 52.9 %all-gather.7.cloned.1.call-start = ((), (), s32[]{:S(2)}) async-start(), calls=%async_computation.4 | async-start | bytes 4718592 | tf_op jit(solution)/shard_map/all_gather | solution.py:85
  14.6 47.2 %copy-start.70 = (f32[384]{0:T(512)S(1)}, f32[384]{0:T(512)}, u32[]{:S(2)}) copy-start(f32[384]{0:T(512)} %param.33) | copy-start | bytes 4612
  14.6 239.8 %reduce-scatter.5.cloned.1.call-start = ((), (), s32[]{:S(2)}) async-start(), calls=%async_computation.5 | async-start | bytes 9437184 | tf_op jit(solution)/shard_map/reduce_scatter | solution.py:132
  239.5 40.5 %all-gather.11.cloned.1.call-start = ((), (), s32[]{:S(2)}) async-start(), calls=%async_computation.7 | async-start | bytes 2949120 | tf_op jit(solution)/shard_map/all_gather | solution.py:73
  241.7 52.5 %all-gather.9.cloned.1.call-start = ((), (), s32[]{:S(2)}) async-start(), calls=%async_computation.6 | async-start | bytes 4718592 | tf_op jit(solution)/shard_map/all_gather | solution.py:135
  260.3 33.8 %copy-start.69 = (f32[1536]{0:T(1024)S(1)}, f32[1536]{0:T(1024)}, u32[]{:S(2)}) copy-start(f32[1536]{0:T(1024)} %param.40) | copy-start | bytes 18436
  260.4 68.6 %all-gather.15.cloned.1.call-start = ((), (), s32[]{:S(2)}) async-start(), calls=%async_computation.10 | async-start | bytes 4718592 | tf_op jit(solution)/shard_map/all_gather | solution.py:148
  261.0 89.0 %all-gather.13.cloned.1.call-start = ((), (), s32[]{:S(2)}) async-start(), calls=%async_computation.8 | async-start | bytes 2949120 | tf_op jit(solution)/shard_map/all_gather | solution.py:75
  261.9 129.9 %reduce-scatter.9.cloned.1.call-start = ((), (), s32[]{:S(2)}) async-start(), calls=%async_computation.11 | async-start | bytes 9437184 | tf_op jit(solution)/shard_map/reduce_scatter | solution.py:165
  350.0 20.3 %copy-start.67 = (bf16[768,1536]{1,0:T(8,128)(2,1)S(1)}, bf16[768,1536]{1,0:T(8,128)(2,1)}, u32[]{:S(2)}) copy-start(bf16[768,1536]{1,0:T(8,128)(2,1)} %all-gather.11.cloned.1.call-done) | copy-start | bytes 7077892
  377.3 28.7 %reduce-scatter.7.cloned.1.call-start = ((), (), s32[]{:S(2)}) async-start(), calls=%async_computation.9 | async-start | bytes 4718592 | tf_op jit(solution)/shard_map/reduce_scatter | solution.py:143
  388.4 37.6 %all-gather.17.cloned.1.call-start = ((), (), s32[]{:S(2)}) async-start(), calls=%async_computation.12 | async-start | bytes 4718592 | tf_op jit(solution)/shard_map/all_gather | solution.py:171
  406.0 20.0 %copy-start.30 = (bf16[384,768]{0,1:T(8,128)(2,1)S(1)}, bf16[384,768]{0,1:T(8,128)(2,1)}, u32[]{:S(2)}) copy-start(bf16[384,768]{0,1:T(8,128)(2,1)} %all_gather.34) | copy-start | bytes 1769476
  412.5 401.7 %reduce-scatter.11.cloned.1.call-start = ((), (), s32[]{:S(2)}) async-start(), calls=%async_computation.13 | async-start | bytes 9437184 | tf_op jit(solution)/shard_map/reduce_scatter | solution.py:242
  793.4 100.4 %all-reduce.7.cloned.1.call-start = ((), (), s32[]{:S(2)}) async-start(), calls=%async_computation.14 | async-start | bytes 6144000 | tf_op jit(solution)/shard_map/psum | solution.py:264
  823.5 479.0 %all-reduce.11.cloned.1.call-start = ((), (), s32[]{:S(2)}) async-start(), calls=%async_computation.16 | async-start | bytes 28311552 | tf_op jit(solution)/shard_map/psum | solution.py:301
  837.3 56.6 %copy-start.59 = (f32[1536]{0:T(1024)S(1)}, f32[1536]{0:T(1024)}, u32[]{:S(2)}) copy-start(f32[1536]{0:T(1024)} %get-tuple-element.344) | copy-start | bytes 18436
  837.3 56.9 %copy-start.10 = (bf16[4,512,6,64]{1,3,2,0:T(8,128)(2,1)S(1)}, bf16[4,512,6,64]{1,3,2,0:T(8,128)(2,1)}, u32[]{:S(2)}) copy-start(bf16[4,512,6,64]{1,3,2,0:T(8,128)(2,1)} %get-tuple-element.179) | copy-start | bytes 4718596
  837.3 57.7 %copy-start.55 = (f32[768]{0:T(1024)S(1)}, f32[768]{0:T(1024)}, u32[]{:S(2)}) copy-start(f32[768]{0:T(1024)} %get-tuple-element.256) | copy-start | bytes 9220
  837.3 57.7 %copy-start.56 = (f32[768]{0:T(1024)S(1)}, f32[768]{0:T(1024)}, u32[]{:S(2)}) copy-start(f32[768]{0:T(1024)} %get-tuple-element.262) | copy-start | bytes 9220
  837.3 57.7 %copy-start.57 = (f32[768]{0:T(1024)S(1)}, f32[768]{0:T(1024)}, u32[]{:S(2)}) copy-start(f32[768]{0:T(1024)} %get-tuple-element.326) | copy-start | bytes 9220
  837.3 57.7 %copy-start.58 = (f32[768]{0:T(1024)S(1)}, f32[768]{0:T(1024)}, u32[]{:S(2)}) copy-start(f32[768]{0:T(1024)} %get-tuple-element.342) | copy-start | bytes 9220
  837.4 585.4 %all-reduce.9.cloned.1.call-start = ((), (), s32[]{:S(2)}) async-start(), calls=%async_computation.15 | async-start | bytes 6144000 | tf_op jit(solution)/shard_map/psum | solution.py:263
  1311.7 114.7 %copy-start.1 = (f32[1000,768]{1,0:T(8,128)S(1)}, f32[1000,768]{1,0:T(8,128)}, u32[]{:S(2)}) copy-start(f32[1000,768]{1,0:T(8,128)} %param.27) | copy-start | bytes 9216004
  (71 other events, 393.7 us)
Sparse Core Ops, SparseCore 0:
  14.7 14.8 all-gather.6
  239.6 14.7 reduce-scatter.4
  412.6 13.3 all-gather.16
  793.5 15.6 reduce-scatter.10
  823.6 70.1 all-reduce.6
  901.2 401.2 all-reduce.10
  1305.0 117.6 all-reduce.8
Sparse Core Ops, SparseCore 1:
  242.4 37.6 all-gather.10
  282.1 12.0 all-gather.8
  295.6 13.2 all-gather.14
  311.4 38.5 all-gather.12
  377.4 14.3 reduce-scatter.8
  394.0 11.9 reduce-scatter.6
